TPU v7x, 256 devices: a whole 4x4x8 slice. The times are simulated.
256 devices in a mesh: tm: 32 (over y, z), row: 8 (over x, core).
Axes of the slice: x: 4, y: 4, z: 8, core: 2. Of those that a mesh axis runs over, the one named last changes fastest.
Arguments:
- precisions: float32 [32, 1024, 1024], P('tm', 'row'), as said below
- couplings: float32 [32, 1024, 1024], P('tm', 'row'), as said below
- right_sides: float32 [32, 1024, 256], P('tm', 'row'), may hold values from -6 to 6
Outputs:
- pivot_blocks: float32 [32, 1024, 1024], P('tm', 'row')
- coupling_blocks: float32 [32, 1024, 1024], P('tm', 'row')
- reduced_sides: float32 [32, 1024, 256], P('tm', 'row')
Inputs may be any that keep to these rules, and one draw needn't show every extreme that they name: precisions and couplings together form a symmetric positive definite block-tridiagonal matrix whose eigenvalues are 1 or more; couplings[0] is zero. `couplings`: see precisions.
All inputs are finite; a program needn't handle non-finite values.
Results may differ from a plain program's by a relative error of at most 0.00023.
Values sent between devices are 32-bit elements; how exact they have to be, the bound alone decides.
No kernel may reach another device: no remote copies, remote signals or barrier semaphores. Data moves between devices by JAX's collectives and lax.ppermute only.
A program may use at most 128 MiB of HBM per device.

v0:
```python
import jax
import jax.numpy as jnp
from jax import lax
from jax.sharding import PartitionSpec as P

LEVELS = 2


def from_behind(block, axis, distance):
    devices = range(lax.axis_size(axis))
    route = [(i - distance, i) for i in devices if i - distance in devices]
    return lax.ppermute(block, axis, route)


def contract(left, right):
    return lax.dot_general(left, right, (((0,), (0,)), ((), ())), precision=lax.Precision.HIGHEST)


def split_cholesky(matrix):
    order = matrix.shape[0]
    if order <= 512:
        return jnp.linalg.cholesky(matrix)
    half = order // 2
    upper_factor = split_cholesky(matrix[:half, :half])
    solved_cols = jax.scipy.linalg.solve_triangular(upper_factor, matrix[:half, half:], lower=True)
    lower_left = solved_cols.T
    remainder = matrix[half:, half:] - contract(solved_cols, solved_cols)
    lower_factor = split_cholesky(remainder)
    top_rows = jnp.concatenate(
        [upper_factor, jnp.zeros((half, order - half), matrix.dtype)], axis=1
    )
    bottom_rows = jnp.concatenate([lower_left, lower_factor], axis=1)
    return jnp.concatenate([top_rows, bottom_rows], axis=0)


def local(precisions, couplings, right_sides):
    diagonal_pivot_rows = precisions[0]
    offdiag_coupling_rows = couplings[0]
    rhs_side_rows = right_sides[0]
    row_count = diagonal_pivot_rows.shape[0]
    block_position = lax.axis_index("tm")
    row_start = lax.axis_index("row") * row_count
    offdiag_coupling_rows = jnp.where(
        block_position == 0, jnp.zeros_like(offdiag_coupling_rows), offdiag_coupling_rows
    )
    for level_step in range(LEVELS):
        level_stride = 1 << level_step
        whole_pivot, whole_coupling, whole_side = (
            lax.all_gather(diagonal_pivot_rows, "row", axis=0, tiled=True),
            lax.all_gather(offdiag_coupling_rows, "row", axis=0, tiled=True),
            lax.all_gather(rhs_side_rows, "row", axis=0, tiled=True),
        )
        next_coupling = from_behind(whole_coupling, "tm", -level_stride)
        factor = split_cholesky(whole_pivot)
        left_part = jax.scipy.linalg.cho_solve((factor, True), offdiag_coupling_rows.T)
        right_cols = lax.dynamic_slice_in_dim(next_coupling, row_start, row_count, 1)
        right_part = jax.scipy.linalg.cho_solve((factor, True), right_cols)
        left_block = lax.dot_general(
            left_part, whole_coupling, (((0,), (1,)), ((), ())), precision=lax.Precision.HIGHEST
        )
        left_side = contract(left_part, whole_side)
        right_block = contract(right_part, next_coupling)
        right_side = contract(right_part, whole_side)
        new_coupling = -contract(left_part, next_coupling)
        received_following = from_behind((left_block, left_side), "tm", -level_stride)
        received_previous = from_behind((right_block, right_side, new_coupling), "tm", level_stride)
        diagonal_pivot_rows = diagonal_pivot_rows - received_following[0] - received_previous[0]
        rhs_side_rows = rhs_side_rows - received_following[1] - received_previous[1]
        offdiag_coupling_rows = received_previous[2]
    return (diagonal_pivot_rows[None], offdiag_coupling_rows[None], rhs_side_rows[None])


def solution(mesh):
    placed = (P("tm", "row", None), P("tm", "row", None), P("tm", "row", None))
    return jax.shard_map(
        local,
        mesh=mesh,
        in_specs=placed,
        out_specs=(P("tm", "row", None), P("tm", "row", None), P("tm", "row", None)),
        check_vma=False,
    )
```

profile of v0, /device:TPU:8, one launch (start us, length us, event | category | flops | bytes accessed | tf_op | source)
XLA Modules:
  0.0 1219.0 jit_solution(4765637610458641546)
XLA Ops:
  13.9 38.0 %all-gather.16.cloned.1.call-done = f32[1,1024,1024]{1,2,0:T(8,128)} async-done(((f32[1,128,1024]{1,2,0:T(8,128)}), f32[1,1024,1024]{1,2,0:T(8,128)}) %all-gather.16.cloned.1.call-update) | async-done | bytes 4194320 | tf_op jit(solution)/shard_map/all_gather | solution.py:49
  55.0 11.7 cholesky.462
  66.7 9.8 custom-call.41
  77.4 11.7 cholesky.481
  89.1 10.0 custom-call.42
  99.8 11.7 cholesky.502
  112.2 9.8 custom-call.43
  122.6 11.7 cholesky.519
  135.0 11.0 compare_reduce_fusion.14
  148.7 7.7 while.12
  156.4 39.3 %custom-call.44 = f32[4,128,128]{1,2,0:T(8,128)S(1)} custom-call(f32[4,128,128]{2,1,0:T(8,128)S(1)} %get-tuple-element.46), custom_call_target="InvertDiagBlocksLowerTriangular" | custom-call | tf_op jit(solution)/shard_map/jit(_solve_triangular)/triangular_solve | solution.py:25
  213.0 11.7 cholesky.534
  225.3 10.2 custom-call.45
  240.0 13.2 %cholesky.553 = f32[128,128]{1,0:T(8,128)} custom-call(f32[128,128]{1,0:T(8,128)} %cholesky.763), custom_call_target="Cholesky" | custom-call | tf_op jit(solution)/shard_map/jit(cholesky)/cholesky | solution.py:22
  255.4 9.8 custom-call.46
  266.8 11.9 cholesky.574
  279.3 9.8 custom-call.47
  290.6 11.7 cholesky.591
  308.1 23.2 %while.13 = (s32[]{:T(128)}, f32[1024,1024]{1,0:T(8,128)}, s32[8,2]{0,1:T(2,128)S(1)}, f32[8,128,128]{2,1,0:T(8,128)S(1)}, s32[]{:T(128)}) while((s32[]{:T(128)}, f32[1024,1024]{1,0:T(8,128)}, s32[8,2]{0,1:T(2,128)S(1)}, f32[8,128,128]{2,1,0:T(8,128)S(1)}, s32[]{:T(128)}) %tuple.193), condition=%wide.while_cond.1, body=%wide.while_body.1.sunk | while | flops 2 | bytes 131181 | solution.py:55
  331.3 78.6 %custom-call.48 = f32[8,128,128]{1,2,0:T(8,128)S(1)} custom-call(f32[8,128,128]{2,1,0:T(8,128)S(1)} %get-tuple-element.47), custom_call_target="InvertDiagBlocksLowerTriangular" | custom-call | tf_op jit(solution)/shard_map/jit(_cho_solve)/triangular_solve | solution.py:55
  410.0 5.7 collective-permute-start.1
  440.3 66.3 %collective-permute-done.1 = f32[1024,1024]{1,0:T(8,128)S(1)} collective-permute-done((f32[1024,1024]{1,0:T(8,128)}, f32[1024,1024]{1,0:T(8,128)S(1)}, u32[]{:S(2)}, u32[]{:S(2)}) %collective-permute-start.1) | collective-permute-done | bytes 4194336 | tf_op jit(solution)/shard_map/ppermute | solution.py:12
  518.1 7.0 fusion.395
  527.6 14.7 %collective-permute-done.2 = f32[128,1024]{0,1:T(8,128)S(1)} collective-permute-done((f32[128,1024]{0,1:T(8,128)S(1)}, f32[128,1024]{0,1:T(8,128)S(1)}, u32[]{:S(2)}, u32[]{:S(2)}) %collective-permute-start.2) | collective-permute-done | bytes 524320 | tf_op jit(solution)/shard_map/ppermute | solution.py:12
  549.8 14.0 %collective-permute-done.3 = f32[128,1024]{1,0:T(8,128)S(1)} collective-permute-done((f32[128,1024]{1,0:T(8,128)S(1)}, f32[128,1024]{1,0:T(8,128)S(1)}, u32[]{:S(2)}, u32[]{:S(2)}) %collective-permute-start.3) | collective-permute-done | bytes 524320 | tf_op jit(solution)/shard_map/ppermute | solution.py:12
  584.0 11.7 cholesky.606
  595.9 9.8 custom-call.50
  606.4 11.7 cholesky.625
  619.4 10.2 custom-call.51
  630.3 11.7 cholesky.646
  642.8 9.8 custom-call.52
  653.2 11.7 cholesky.663
  668.6 7.6 while.14
  676.2 39.3 %custom-call.53 = f32[4,128,128]{1,2,0:T(8,128)S(1)} custom-call(f32[4,128,128]{2,1,0:T(8,128)S(1)} %get-tuple-element.49), custom_call_target="InvertDiagBlocksLowerTriangular" | custom-call | tf_op jit(solution)/shard_map/jit(_solve_triangular)/triangular_solve | solution.py:25
  732.0 11.7 cholesky.678
  744.3 10.0 custom-call.54
  758.8 13.2 %cholesky.697 = f32[128,128]{1,0:T(8,128)} custom-call(f32[128,128]{1,0:T(8,128)} %cholesky.789), custom_call_target="Cholesky" | custom-call | tf_op jit(solution)/shard_map/jit(cholesky)/cholesky | solution.py:22
  774.2 9.8 custom-call.55
  785.5 12.1 cholesky.718
  798.3 9.8 custom-call.56
  809.6 11.7 cholesky.735
  827.1 22.7 %while.15 = (s32[]{:T(128)}, f32[1024,1024]{1,0:T(8,128)}, s32[8,2]{0,1:T(2,128)S(1)}, f32[8,128,128]{2,1,0:T(8,128)S(1)}, s32[]{:T(128)}) while((s32[]{:T(128)}, f32[1024,1024]{1,0:T(8,128)}, s32[8,2]{0,1:T(2,128)S(1)}, f32[8,128,128]{2,1,0:T(8,128)S(1)}, s32[]{:T(128)}) %tuple.216), condition=%wide.while_cond.1.clone.1, body=%wide.while_body.1.clone.1.sunk | while | flops 2 | bytes 131181 | solution.py:55
  849.8 78.8 %custom-call.57 = f32[8,128,128]{1,2,0:T(8,128)S(1)} custom-call(f32[8,128,128]{2,1,0:T(8,128)S(1)} %get-tuple-element.50), custom_call_target="InvertDiagBlocksLowerTriangular" | custom-call | tf_op jit(solution)/shard_map/jit(_cho_solve)/triangular_solve | solution.py:55
  951.6 5.6 collective-permute-start.5
  977.8 174.4 %collective-permute-done.5 = f32[1024,1024]{1,0:T(8,128)} collective-permute-done((f32[1024,1024]{1,0:T(8,128)}, f32[1024,1024]{1,0:T(8,128)}, u32[]{:S(2)}, u32[]{:S(2)}) %collective-permute-start.5) | collective-permute-done | bytes 4194336 | tf_op jit(solution)/shard_map/ppermute | solution.py:12
  1175.2 5.5 collective-permute-start.7
  1180.6 8.5 fusion.397
  1198.4 10.8 collective-permute-done.11
  (496 shorter events, 284.3 us)
Async XLA Ops:
  7.2 44.7 %all-gather.16.cloned.1.call-start = ((), (), s32[]{:S(2)}) async-start(), calls=%async_computation.3 | async-start | bytes 4718592 | tf_op jit(solution)/shard_map/all_gather | solution.py:49
  9.3 400.7 %all-gather.18.cloned.1.call-start = ((), (), s32[]{:S(2)}) async-start(), calls=%async_computation.4 | async-start | bytes 4718592 | tf_op jit(solution)/shard_map/all_gather | solution.py:50
  11.2 553.5 %all-gather.20.cloned.1.call-start = ((), (), s32[]{:S(2)}) async-start(), calls=%async_computation.5 | async-start | bytes 1179648 | tf_op jit(solution)/shard_map/all_gather | solution.py:51
  12.0 568.9 %all-gather.10.cloned.1.call-start = ((), (), s32[]{:S(2)}) async-start(), calls=%async_computation | async-start | bytes 4718592 | tf_op jit(solution)/shard_map/all_gather | solution.py:49
  195.7 5.8 copy-start.18
  204.3 1.4 copy-start.9
  204.4 1.3 copy-start.11
  212.0 1.0 copy-start.7
  224.7 0.6 copy-start.19
  305.5 110.1 %copy-start.15 = (f32[1024,128]{0,1:T(8,128)S(1)}, f32[1024,128]{0,1:T(8,128)}, u32[]{:S(2)}) copy-start(f32[1024,128]{0,1:T(8,128)} %fusion.497) | copy-start | bytes 1572868
  410.0 14.6 %copy-start.1 = (f32[1024,1024]{1,0:T(8,128)S(1)}, f32[1024,1024]{1,0:T(8,128)}, u32[]{:S(2)}) copy-start(f32[1024,1024]{1,0:T(8,128)} %get-tuple-element.458) | copy-start | bytes 12582916
  410.0 96.7 %collective-permute-start.1 = (f32[1024,1024]{1,0:T(8,128)}, f32[1024,1024]{1,0:T(8,128)S(1)}, u32[]{:S(2)}, u32[]{:S(2)}) collective-permute-start(f32[1024,1024]{1,0:T(8,128)} %bitcast.470), channel_id=1, source_target_pairs={{8,0},{16,8},{24,16},{32,24},{40,32},{48,40},{56,48},{64,56},{72,6... | collective-permute-start | bytes 12582920 | tf_op jit(solution)/shard_map/ppermute | solution.py:12
  428.0 5.2 copy-start.5
  437.0 90.6 %collective-permute-start = (f32[128,1024]{0,1:T(8,128)S(1)}, f32[128,1024]{0,1:T(8,128)S(1)}, u32[]{:S(2)}, u32[]{:S(2)}) collective-permute-start(f32[128,1024]{0,1:T(8,128)S(1)} %fusion.389), channel_id=1, source_target_pairs={{8,0},{16,8},{24,16},{32,24},{40,32},{48,40},{56,48},{64,56},{72,6... | collective-permute-start | bytes 1572872 | tf_op jit(solution)/shard_map/ppermute | solution.py:12
  506.6 11.4 copy-start.2
  516.5 25.8 %copy-start.3 = (f32[1,128,1024]{1,2,0:T(8,128)S(1)}, f32[1,128,1024]{1,2,0:T(8,128)}, u32[]{:S(2)}) copy-start(f32[1,128,1024]{1,2,0:T(8,128)} %copy.6) | copy-start | bytes 1572868
  525.1 17.3 %collective-permute-start.2 = (f32[128,1024]{0,1:T(8,128)S(1)}, f32[128,1024]{0,1:T(8,128)S(1)}, u32[]{:S(2)}, u32[]{:S(2)}) collective-permute-start(f32[128,1024]{0,1:T(8,128)S(1)} %fusion.395), channel_id=1, source_target_pairs={{0,8},{8,16},{16,24},{24,32},{32,40},{40,48},{48,56},{56,64},{64,7... | collective-permute-start | bytes 1572872 | tf_op jit(solution)/shard_map/ppermute | solution.py:12
  543.2 37.0 %copy-start.17 = (f32[1,128,256]{2,1,0:T(8,128)S(1)}, f32[1,128,256]{2,1,0:T(8,128)}, u32[]{:S(2)}) copy-start(f32[1,128,256]{2,1,0:T(8,128)} %param.10) | copy-start | bytes 393220
  543.2 408.4 %all-gather.12.cloned.1.call-start = ((), (), s32[]{:S(2)}) async-start(), calls=%async_computation.1 | async-start | bytes 4718592 | tf_op jit(solution)/shard_map/all_gather | solution.py:50
  547.9 16.0 %collective-permute-start.3 = (f32[128,1024]{1,0:T(8,128)S(1)}, f32[128,1024]{1,0:T(8,128)S(1)}, u32[]{:S(2)}, u32[]{:S(2)}) collective-permute-start(f32[128,1024]{1,0:T(8,128)S(1)} %convolution_negate_fusion.1), channel_id=1, source_target_pairs={{0,8},{8,16},{16,24},{24,32},{32,40},{40,48},{48,56},{56,64},{64,7... | collective-permute-start | bytes 1572872 | tf_op jit(solution)/shard_map/ppermute | solution.py:12
  563.9 0.8 copy-start.13
  564.7 398.9 %all-gather.14.cloned.1.call-start = ((), (), s32[]{:S(2)}) async-start(), calls=%async_computation.2 | async-start | bytes 1179648 | tf_op jit(solution)/shard_map/all_gather | solution.py:51
  567.0 8.3 collective-permute-start.8
  571.2 9.0 collective-permute-start.9
  715.5 5.8 copy-start.21
  723.0 1.6 copy-start.10
  723.2 1.5 copy-start.12
  731.0 1.0 copy-start.8
  743.7 0.6 copy-start.20
  827.1 111.4 %copy-start.14 = (f32[128,1024]{1,0:T(8,128)S(1)}, f32[128,1024]{1,0:T(8,128)}, u32[]{:S(2)}) copy-start(f32[128,1024]{1,0:T(8,128)} %copy-done.13) | copy-start | bytes 1572868
  951.6 200.6 %collective-permute-start.5 = (f32[1024,1024]{1,0:T(8,128)}, f32[1024,1024]{1,0:T(8,128)}, u32[]{:S(2)}, u32[]{:S(2)}) collective-permute-start(f32[1024,1024]{1,0:T(8,128)} %all-gather.12.cloned.1.call-done), channel_id=1, source_target_pairs={{16,0},{24,8},{32,16},{40,24},{48,32},{56,40},{64,48},{72,56},{80,... | collective-permute-start | bytes 12582920 | tf_op jit(solution)/shard_map/ppermute | solution.py:12
  963.6 189.8 %copy-start = (f32[1024,1024]{1,0:T(8,128)S(1)}, f32[1024,1024]{1,0:T(8,128)}, u32[]{:S(2)}) copy-start(f32[1024,1024]{1,0:T(8,128)} %get-tuple-element.457) | copy-start | bytes 12582916
  966.0 232.4 %collective-permute-start.10 = (f32[128,256]{1,0:T(8,128)S(1)}, f32[128,256]{1,0:T(8,128)S(1)}, u32[]{:S(2)}, u32[]{:S(2)}) collective-permute-start(f32[128,256]{1,0:T(8,128)S(1)} %fusion.398), channel_id=1, source_target_pairs={{16,0},{24,8},{32,16},{40,24},{48,32},{56,40},{64,48},{72,56},{80,... | collective-permute-start | bytes 393224 | tf_op jit(solution)/shard_map/ppermute | solution.py:12
  975.3 234.5 %collective-permute-start.4 = (f32[128,1024]{0,1:T(8,128)S(1)}, f32[128,1024]{0,1:T(8,128)S(1)}, u32[]{:S(2)}, u32[]{:S(2)}) collective-permute-start(f32[128,1024]{0,1:T(8,128)S(1)} %fusion.396), channel_id=1, source_target_pairs={{16,0},{24,8},{32,16},{40,24},{48,32},{56,40},{64,48},{72,56},{80,... | collective-permute-start | bytes 1572872 | tf_op jit(solution)/shard_map/ppermute | solution.py:12
  1170.5 22.7 %copy-start.6 = (f32[1024,256]{1,0:T(8,128)S(1)}, f32[1024,256]{1,0:T(8,128)}, u32[]{:S(2)}) copy-start(f32[1024,256]{1,0:T(8,128)} %all-gather.14.cloned.1.call-done) | copy-start | bytes 3145732
  1175.1 34.0 %copy-start.16 = (f32[128,256]{1,0:T(8,128)S(1)}, f32[128,256]{1,0:T(8,128)}, u32[]{:S(2)}) copy-start(f32[128,256]{1,0:T(8,128)} %fusion.247) | copy-start | bytes 393220
  1175.2 34.7 %copy-start.4 = (f32[128,1024]{0,1:T(8,128)S(1)}, f32[128,1024]{0,1:T(8,128)}, u32[]{:S(2)}) copy-start(f32[128,1024]{0,1:T(8,128)} %fusion.33) | copy-start | bytes 1572868
  1175.2 34.7 %collective-permute-start.7 = (f32[128,1024]{1,0:T(8,128)S(1)}, f32[128,1024]{1,0:T(8,128)S(1)}, u32[]{:S(2)}, u32[]{:S(2)}) collective-permute-start(f32[128,1024]{1,0:T(8,128)S(1)} %convolution_negate_fusion), channel_id=1, source_target_pairs={{0,16},{8,24},{16,32},{24,40},{32,48},{40,56},{48,64},{56,72},{64,... | collective-permute-start | bytes 1572872 | tf_op jit(solution)/shard_map/ppermute | solution.py:12
  1189.1 20.7 %collective-permute-start.6 = (f32[128,1024]{0,1:T(8,128)S(1)}, f32[128,1024]{0,1:T(8,128)S(1)}, u32[]{:S(2)}, u32[]{:S(2)}) collective-permute-start(f32[128,1024]{0,1:T(8,128)S(1)} %fusion.397), channel_id=1, source_target_pairs={{0,16},{8,24},{16,32},{24,40},{32,48},{40,56},{48,64},{56,72},{64,... | collective-permute-start | bytes 1572872 | tf_op jit(solution)/shard_map/ppermute | solution.py:12
  1194.2 15.0 %collective-permute-start.11 = (f32[128,256]{1,0:T(8,128)S(1)}, f32[128,256]{1,0:T(8,128)S(1)}, u32[]{:S(2)}, u32[]{:S(2)}) collective-permute-start(f32[128,256]{1,0:T(8,128)S(1)} %fusion.399), channel_id=1, source_target_pairs={{0,16},{8,24},{16,32},{24,40},{32,48},{40,56},{48,64},{56,72},{64,... | collective-permute-start | bytes 393224 | tf_op jit(solution)/shard_map/ppermute | solution.py:12
Sparse Core Ops, SparseCore 0:
  10.4 41.4 all-gather.15
  53.8 35.9 all-gather.17
  91.6 25.9 all-gather.19
  543.3 37.1 all-gather.9
  582.8 35.7 all-gather.11
  620.9 26.0 all-gather.13
where the time goes:
time: 1230 us; the launch traced here: 1220 us
  other arithmetic  586 us (48%)
  waiting for transfers between devices  324 us (26%)
  matrix products  156 us (13%)
  local copies, waits for them, and re-layouts  79.8 us (6%)
  starting transfers between devices  45.5 us (4%)
  between operations  27.1 us (2%)
    another operation x59, other arithmetic, split_cholesky(): return jnp.linalg.cholesky(matrix)  332 us
    ppermute x12, waiting for transfers between devices, from_behind(): return lax.ppermute(block, axis, route)  285 us
    another operation x5, other arithmetic, local(): jax.scipy.linalg.cho_solve((factor, True), offdiag_coupling_rows.T)  162 us
    another operation x5, other arithmetic, split_cholesky(): jax.scipy.linalg.solve_triangular(upper_factor, matrix[:half, half:], low...  79.2 us
    another operation x59, local copies, waits for them, and re-layouts, local(): jax.scipy.linalg.cho_solve((factor, True), offdiag_coupling_rows.T)  45.7 us
    another operation x60, matrix products, local(): jax.scipy.linalg.cho_solve((factor, True), offdiag_coupling_rows.T)  45.7 us
    ppermute x12, starting transfers between devices, from_behind(): return lax.ppermute(block, axis, route)  45.2 us
    dot_general x10, matrix products, contract(): lax.dot_general(left, right, (((0,), (0,)), ((), ())), precision=lax.Prec...  39.6 us
  transfers between devices with their start and end apart: 18, of which 7 were waited for; matrix products, arithmetic and copies ran while one was open for 67% of the time, Pallas kernels for 0%

commit v1 on v0

--- a/solution.py
+++ b/solution.py
@@ -46,7 +46,12 @@
     for level_step in range(LEVELS):
         level_stride = 1 << level_step
         whole_pivot, whole_coupling, whole_side = (
-            lax.all_gather(diagonal_pivot_rows, "row", axis=0, tiled=True),
+            jnp.concatenate(
+                lax.all_to_all(
+                    jnp.stack([diagonal_pivot_rows] * lax.axis_size("row")), "row", 0, 0
+                ),
+                axis=0,
+            ),
             lax.all_gather(offdiag_coupling_rows, "row", axis=0, tiled=True),
             lax.all_gather(rhs_side_rows, "row", axis=0, tiled=True),
         )

time: 1230 us -> 1320 us (1.073)
  waiting for transfers between devices: 324 us -> 397 us
  local copies, waits for them, and re-layouts: 79.8 us -> 93.3 us
    all_to_all x0 -> x2, waiting for transfers between devices: none -> 102 us  [local(): lax.all_to_all(jnp.stack([diagonal_pivot_rows] * lax.axis_size('row')), '...]
    all_gather x2 -> x0, waiting for transfers between devices: 38 us -> none  [local(): lax.all_gather(diagonal_pivot_rows, 'row', axis=0, tiled=True)]
  transfers between devices with their start and end apart: 18 -> 18, of which waited for: 7 -> 8; matrix products, arithmetic and copies ran while one was open for 67% -> 63% of each run, Pallas kernels for 0% -> 0%
where the time goes in v1:
time: 1320 us; the launch traced here: 1310 us
  other arithmetic  578 us (44%)
  waiting for transfers between devices  397 us (30%)
  matrix products  158 us (12%)
  local copies, waits for them, and re-layouts  93.3 us (7%)
  starting transfers between devices  52.1 us (4%)
  between operations  27.4 us (2%)
    another operation x59, other arithmetic, split_cholesky(): return jnp.linalg.cholesky(matrix)  320 us
    ppermute x12, waiting for transfers between devices, from_behind(): return lax.ppermute(block, axis, route)  294 us
    another operation x5, other arithmetic, local(): jax.scipy.linalg.cho_solve((factor, True), offdiag_coupling_rows.T)  164 us
    all_to_all x2, waiting for transfers between devices, local(): lax.all_to_all(jnp.stack([diagonal_pivot_rows] * lax.axis_size('row')), '...  102 us
    another operation x5, other arithmetic, split_cholesky(): jax.scipy.linalg.solve_triangular(upper_factor, matrix[:half, half:], low...  80.2 us
    another operation x60, matrix products, local(): jax.scipy.linalg.cho_solve((factor, True), offdiag_coupling_rows.T)  50.8 us
    another operation x59, local copies, waits for them, and re-layouts, local(): jax.scipy.linalg.cho_solve((factor, True), offdiag_coupling_rows.T)  46.6 us
    ppermute x12, starting transfers between devices, from_behind(): return lax.ppermute(block, axis, route)  42.6 us
  transfers between devices with their start and end apart: 18, of which 8 were waited for; matrix products, arithmetic and copies ran while one was open for 63% of the time, Pallas kernels for 0%

profile of v1, /device:TPU:8, one launch (start us, length us, event | category | flops | bytes accessed | tf_op | source)
XLA Modules:
  0.0 1305.3 jit_solution(3608266439759682838)
XLA Ops:
  19.0 64.9 %all-to-all-done = f32[8,128,1024]{1,2,0:T(8,128)} async-done(((f32[8,128,1024]{1,2,0:T(8,128)}), f32[8,128,1024]{1,2,0:T(8,128)}, u32[]{:S(2)}, u32[]{:S(2)}) %all-to-all-start) | async-done | bytes 4194336 | tf_op jit(solution)/shard_map/all_to_all | solution.py:50
  90.5 11.7 cholesky.462
  102.2 9.8 custom-call.41
  112.9 11.7 cholesky.481
  124.6 10.0 custom-call.42
  135.2 11.7 cholesky.502
  147.7 9.8 custom-call.43
  158.1 12.1 cholesky.519
  174.4 8.1 while.12
  182.6 39.3 %custom-call.44 = f32[4,128,128]{1,2,0:T(8,128)S(1)} custom-call(f32[4,128,128]{2,1,0:T(8,128)S(1)} %get-tuple-element.46), custom_call_target="InvertDiagBlocksLowerTriangular" | custom-call | tf_op jit(solution)/shard_map/jit(_solve_triangular)/triangular_solve | solution.py:25
  239.2 11.7 cholesky.534
  251.5 10.0 custom-call.45
  266.0 13.2 %cholesky.553 = f32[128,128]{1,0:T(8,128)} custom-call(f32[128,128]{1,0:T(8,128)} %cholesky.763), custom_call_target="Cholesky" | custom-call | tf_op jit(solution)/shard_map/jit(cholesky)/cholesky | solution.py:22
  281.4 9.8 custom-call.46
  292.8 11.9 cholesky.574
  305.4 9.8 custom-call.47
  316.7 11.7 cholesky.591
  334.5 24.2 %while.13 = (s32[]{:T(128)}, f32[1024,1024]{1,0:T(8,128)}, s32[8,2]{0,1:T(2,128)S(1)}, f32[8,128,128]{2,1,0:T(8,128)S(1)}, s32[]{:T(128)}) while((s32[]{:T(128)}, f32[1024,1024]{1,0:T(8,128)}, s32[8,2]{0,1:T(2,128)S(1)}, f32[8,128,128]{2,1,0:T(8,128)S(1)}, s32[]{:T(128)}) %tuple.192), condition=%wide.while_cond.1, body=%wide.while_body.1.sunk | while | flops 2 | bytes 131181 | solution.py:60
  358.6 78.8 %custom-call.48 = f32[8,128,128]{1,2,0:T(8,128)S(1)} custom-call(f32[8,128,128]{2,1,0:T(8,128)S(1)} %get-tuple-element.47), custom_call_target="InvertDiagBlocksLowerTriangular" | custom-call | tf_op jit(solution)/shard_map/jit(_cho_solve)/triangular_solve | solution.py:60
  458.1 8.4 collective-permute-start.1
  471.9 6.7 fusion.384
  481.6 75.7 %collective-permute-done.1 = f32[1024,1024]{1,0:T(8,128)S(1)} collective-permute-done((f32[1024,1024]{1,0:T(8,128)}, f32[1024,1024]{1,0:T(8,128)S(1)}, u32[]{:S(2)}, u32[]{:S(2)}) %collective-permute-start.1) | collective-permute-done | bytes 4194336 | tf_op jit(solution)/shard_map/ppermute | solution.py:12
  570.9 11.8 collective-permute-done.3
  592.4 12.6 collective-permute-done.2
  624.2 5.3 collective-permute-done.9
  630.2 36.9 %all-to-all-done.1 = f32[8,128,1024]{1,2,0:T(8,128)} async-done(((f32[8,128,1024]{1,2,0:T(8,128)}), f32[8,128,1024]{1,2,0:T(8,128)}, u32[]{:S(2)}, u32[]{:S(2)}) %all-to-all-start.1) | async-done | bytes 4194336 | tf_op jit(solution)/shard_map/all_to_all | solution.py:50
  673.8 11.7 cholesky.606
  685.7 9.8 custom-call.50
  696.2 11.7 cholesky.625
  709.3 9.9 custom-call.51
  719.9 11.7 cholesky.646
  732.4 9.8 custom-call.52
  742.8 12.1 cholesky.663
  759.7 12.0 while.14
  771.7 39.3 %custom-call.53 = f32[4,128,128]{1,2,0:T(8,128)S(1)} custom-call(f32[4,128,128]{2,1,0:T(8,128)S(1)} %get-tuple-element.49), custom_call_target="InvertDiagBlocksLowerTriangular" | custom-call | tf_op jit(solution)/shard_map/jit(_solve_triangular)/triangular_solve | solution.py:25
  829.1 11.7 cholesky.678
  840.9 10.0 custom-call.54
  853.9 11.7 cholesky.697
  866.9 9.8 custom-call.55
  878.3 12.1 cholesky.718
  891.1 9.8 custom-call.56
  902.4 11.7 cholesky.735
  921.3 22.6 %while.15 = (s32[]{:T(128)}, f32[1024,1024]{1,0:T(8,128)}, s32[8,2]{0,1:T(2,128)S(1)}, f32[8,128,128]{2,1,0:T(8,128)S(1)}, s32[]{:T(128)}) while((s32[]{:T(128)}, f32[1024,1024]{1,0:T(8,128)}, s32[8,2]{0,1:T(2,128)S(1)}, f32[8,128,128]{2,1,0:T(8,128)S(1)}, s32[]{:T(128)}) %tuple.211), condition=%wide.while_cond.1.clone.1, body=%wide.while_body.1.clone.1.sunk | while | flops 2 | bytes 131181 | solution.py:60
  943.9 78.8 %custom-call.57 = f32[8,128,128]{1,2,0:T(8,128)S(1)} custom-call(f32[8,128,128]{2,1,0:T(8,128)S(1)} %get-tuple-element.50), custom_call_target="InvertDiagBlocksLowerTriangular" | custom-call | tf_op jit(solution)/shard_map/jit(_cho_solve)/triangular_solve | solution.py:60
  1056.6 6.7 fusion.391
  1065.7 174.7 %collective-permute-done.5 = f32[1024,1024]{1,0:T(8,128)} collective-permute-done((f32[1024,1024]{1,0:T(8,128)}, f32[1024,1024]{1,0:T(8,128)}, u32[]{:S(2)}, u32[]{:S(2)}) %collective-permute-start.5) | collective-permute-done | bytes 4194336 | tf_op jit(solution)/shard_map/ppermute | solution.py:12
  1276.5 5.5 collective-permute-start.11
  1282.0 13.9 %collective-permute-done.11 = f32[128,256]{1,0:T(8,128)S(1)} collective-permute-done((f32[128,256]{1,0:T(8,128)S(1)}, f32[128,256]{1,0:T(8,128)S(1)}, u32[]{:S(2)}, u32[]{:S(2)}) %collective-permute-start.11) | collective-permute-done | bytes 131104 | tf_op jit(solution)/shard_map/ppermute | solution.py:12
  (494 shorter events, 309.8 us)
Async XLA Ops:
  7.2 450.9 %all-gather.11.cloned.1.call-start = ((), (), s32[]{:S(2)}) async-start(), calls=%async_computation.4 | async-start | bytes 4718592 | tf_op jit(solution)/shard_map/all_gather | solution.py:55
  12.6 5.5 copy-start.13
  12.6 71.2 %all-to-all-start = ((f32[8,128,1024]{1,2,0:T(8,128)}), f32[8,128,1024]{1,2,0:T(8,128)}, u32[]{:S(2)}, u32[]{:S(2)}) async-start(f32[8,128,1024]{1,2,0:T(8,128)} %stack.4), calls=%async_computation | async-start | bytes 8388608 | tf_op jit(solution)/shard_map/all_to_all | solution.py:50
  17.3 596.1 %all-gather.13.cloned.1.call-start = ((), (), s32[]{:S(2)}) async-start(), calls=%async_computation.5 | async-start | bytes 1179648 | tf_op jit(solution)/shard_map/all_gather | solution.py:56
  18.1 1024.3 %all-gather.7.cloned.1.call-start = ((), (), s32[]{:S(2)}) async-start(), calls=%async_computation.2 | async-start | bytes 4718592 | tf_op jit(solution)/shard_map/all_gather | solution.py:55
  86.6 2.0 copy-start.4
  221.9 5.8 copy-start.17
  230.4 1.4 copy-start.9
  230.6 1.3 copy-start.10
  238.2 1.0 copy-start.7
  250.9 0.6 copy-start.19
  458.0 12.6 copy-start.1
  458.1 99.3 %collective-permute-start.1 = (f32[1024,1024]{1,0:T(8,128)}, f32[1024,1024]{1,0:T(8,128)S(1)}, u32[]{:S(2)}, u32[]{:S(2)}) collective-permute-start(f32[1024,1024]{1,0:T(8,128)} %bitcast.480), channel_id=1, source_target_pairs={{8,0},{16,8},{24,16},{32,24},{40,32},{48,40},{56,48},{64,56},{72,6... | collective-permute-start | bytes 12582920 | tf_op jit(solution)/shard_map/ppermute | solution.py:12
  478.5 113.9 %collective-permute-start = (f32[128,1024]{1,0:T(8,128)S(1)}, f32[128,1024]{1,0:T(8,128)}, u32[]{:S(2)}, u32[]{:S(2)}) collective-permute-start(f32[128,1024]{1,0:T(8,128)S(1)} %fusion.384), channel_id=1, source_target_pairs={{8,0},{16,8},{24,16},{32,24},{40,32},{48,40},{56,48},{64,56},{72,6... | collective-permute-start | bytes 1572872 | tf_op jit(solution)/shard_map/ppermute | solution.py:12
  557.3 7.2 copy-start.2
  566.9 15.8 %collective-permute-start.3 = (f32[128,1024]{1,0:T(8,128)S(1)}, f32[128,1024]{1,0:T(8,128)S(1)}, u32[]{:S(2)}, u32[]{:S(2)}) collective-permute-start(f32[128,1024]{1,0:T(8,128)S(1)} %convolution_negate_fusion.1), channel_id=1, source_target_pairs={{0,8},{8,16},{16,24},{24,32},{32,40},{40,48},{48,56},{56,64},{64,7... | collective-permute-start | bytes 1572872 | tf_op jit(solution)/shard_map/ppermute | solution.py:12
  582.7 0.8 copy-start.11
  583.5 4.5 copy-start.3
  585.5 19.5 %copy-start.14 = (f32[1,128,1024]{2,1,0:T(8,128)S(1)}, f32[1,128,1024]{2,1,0:T(8,128)}, u32[]{:S(2)}) copy-start(f32[1,128,1024]{2,1,0:T(8,128)} %param.8) | copy-start | bytes 1572868
  590.5 14.5 %collective-permute-start.2 = (f32[128,1024]{1,0:T(8,128)S(1)}, f32[128,1024]{1,0:T(8,128)S(1)}, u32[]{:S(2)}, u32[]{:S(2)}) collective-permute-start(f32[128,1024]{1,0:T(8,128)S(1)} %fusion.390), channel_id=1, source_target_pairs={{0,8},{8,16},{16,24},{24,32},{32,40},{40,48},{48,56},{56,64},{64,7... | collective-permute-start | bytes 1572872 | tf_op jit(solution)/shard_map/ppermute | solution.py:12
  608.6 20.9 %copy-start.16 = (f32[1,128,256]{2,1,0:T(8,128)S(1)}, f32[1,128,256]{2,1,0:T(8,128)}, u32[]{:S(2)}) copy-start(f32[1,128,256]{2,1,0:T(8,128)} %param.10) | copy-start | bytes 393220
  608.6 58.6 %all-to-all-start.1 = ((f32[8,128,1024]{1,2,0:T(8,128)}), f32[8,128,1024]{1,2,0:T(8,128)}, u32[]{:S(2)}, u32[]{:S(2)}) async-start(f32[8,128,1024]{1,2,0:T(8,128)} %stack.5), calls=%async_computation.1 | async-start | bytes 8388608 | tf_op jit(solution)/shard_map/all_to_all | solution.py:50
  613.3 437.3 %all-gather.9.cloned.1.call-start = ((), (), s32[]{:S(2)}) async-start(), calls=%async_computation.3 | async-start | bytes 1179648 | tf_op jit(solution)/shard_map/all_gather | solution.py:56
  615.7 8.5 collective-permute-start.8
  619.9 9.7 collective-permute-start.9
  669.9 2.0 copy-start.5
  811.0 5.9 copy-start.18
  828.1 1.0 copy-start.8
  917.5 105.2 %copy-start.12 = (f32[128,1024]{1,0:T(8,128)S(1)}, f32[128,1024]{1,0:T(8,128)}, u32[]{:S(2)}) copy-start(f32[128,1024]{1,0:T(8,128)} %copy-done.11) | copy-start | bytes 1572868
  1042.3 198.1 %collective-permute-start.5 = (f32[1024,1024]{1,0:T(8,128)}, f32[1024,1024]{1,0:T(8,128)}, u32[]{:S(2)}, u32[]{:S(2)}) collective-permute-start(f32[1024,1024]{1,0:T(8,128)} %all-gather.7.cloned.1.call-done), channel_id=1, source_target_pairs={{16,0},{24,8},{32,16},{40,24},{48,32},{56,40},{64,48},{72,56},{80,... | collective-permute-start | bytes 12582920 | tf_op jit(solution)/shard_map/ppermute | solution.py:12
  1050.6 190.9 %copy-start = (f32[1024,1024]{1,0:T(8,128)S(1)}, f32[1024,1024]{1,0:T(8,128)}, u32[]{:S(2)}) copy-start(f32[1024,1024]{1,0:T(8,128)} %get-tuple-element.452) | copy-start | bytes 12582916
  1053.0 229.0 %collective-permute-start.10 = (f32[128,256]{1,0:T(8,128)S(1)}, f32[128,256]{1,0:T(8,128)S(1)}, u32[]{:S(2)}, u32[]{:S(2)}) collective-permute-start(f32[128,256]{1,0:T(8,128)S(1)} %fusion.393), channel_id=1, source_target_pairs={{16,0},{24,8},{32,16},{40,24},{48,32},{56,40},{64,48},{72,56},{80,... | collective-permute-start | bytes 393224 | tf_op jit(solution)/shard_map/ppermute | solution.py:12
  1063.2 233.3 %collective-permute-start.4 = (f32[128,1024]{1,0:T(8,128)S(1)}, f32[128,1024]{1,0:T(8,128)S(1)}, u32[]{:S(2)}, u32[]{:S(2)}) collective-permute-start(f32[128,1024]{1,0:T(8,128)S(1)} %fusion.391), channel_id=1, source_target_pairs={{16,0},{24,8},{32,16},{40,24},{48,32},{56,40},{64,48},{72,56},{80,... | collective-permute-start | bytes 1572872 | tf_op jit(solution)/shard_map/ppermute | solution.py:12
  1258.6 16.8 %copy-start.6 = (f32[1024,256]{1,0:T(8,128)S(1)}, f32[1024,256]{1,0:T(8,128)}, u32[]{:S(2)}) copy-start(f32[1024,256]{1,0:T(8,128)} %all-gather.9.cloned.1.call-done) | copy-start | bytes 3145732
  1263.3 32.6 %copy-start.15 = (f32[128,256]{1,0:T(8,128)S(1)}, f32[128,256]{1,0:T(8,128)}, u32[]{:S(2)}) copy-start(f32[128,256]{1,0:T(8,128)} %fusion.240) | copy-start | bytes 393220
  1263.3 33.3 %collective-permute-start.7 = (f32[128,1024]{1,0:T(8,128)S(1)}, f32[128,1024]{1,0:T(8,128)S(1)}, u32[]{:S(2)}, u32[]{:S(2)}) collective-permute-start(f32[128,1024]{1,0:T(8,128)S(1)} %convolution_negate_fusion), channel_id=1, source_target_pairs={{0,16},{8,24},{16,32},{24,40},{32,48},{40,56},{48,64},{56,72},{64,... | collective-permute-start | bytes 1572872 | tf_op jit(solution)/shard_map/ppermute | solution.py:12
  1271.8 24.8 %collective-permute-start.6 = (f32[128,1024]{1,0:T(8,128)S(1)}, f32[128,1024]{1,0:T(8,128)S(1)}, u32[]{:S(2)}, u32[]{:S(2)}) collective-permute-start(f32[128,1024]{1,0:T(8,128)S(1)} %fusion.392), channel_id=1, source_target_pairs={{0,16},{8,24},{16,32},{24,40},{32,48},{40,56},{48,64},{56,72},{64,... | collective-permute-start | bytes 1572872 | tf_op jit(solution)/shard_map/ppermute | solution.py:12
  1276.5 19.4 %collective-permute-start.11 = (f32[128,256]{1,0:T(8,128)S(1)}, f32[128,256]{1,0:T(8,128)S(1)}, u32[]{:S(2)}, u32[]{:S(2)}) collective-permute-start(f32[128,256]{1,0:T(8,128)S(1)} %fusion.394), channel_id=1, source_target_pairs={{0,16},{8,24},{16,32},{24,40},{32,48},{40,56},{48,64},{56,72},{64,... | collective-permute-start | bytes 393224 | tf_op jit(solution)/shard_map/ppermute | solution.py:12
Sparse Core Ops, SparseCore 0:
  10.4 59.2 all-gather.10
  71.6 25.5 all-gather.12
  583.7 31.5 all-gather.6
  630.4 25.9 all-gather.8
